TPU v7x, 32 devices: a whole 2x2x4 slice. The times are simulated.
32 devices in a mesh: space: 16 (over z, x, core), sample: 2 (over y).
Axes of the slice: x: 2, y: 2, z: 4, core: 2. Of those that a mesh axis runs over, the one named last changes fastest.
Arguments:
- spectra: float32 [36, 2, 512, 256], P('sample', None, 'space'), may hold values from -6 to 6
- plane_assign: int32 [2, 18], P('sample'), may hold values from 0 to 17, each once within a row
- fine_state: bfloat16 [4, 32, 131072], P('sample', 'space'), may hold values from 0.3984375 to 1.3984375
- partner_state: float32 [4, 4, 2048], P('sample'), may hold values from 0.4 to 1.4
- coarse_state: float32 [32, 4, 2048], P(('space', 'sample')), may hold values from 0.4 to 1.4
- turbine_x: int32 [16], replicated, may hold values from 0 to 31
- turbine_y: int32 [16], replicated, may hold values from 0 to 62
- turbine_z: int32 [16], replicated, may hold values from 0 to 30
- thrust: float32 [16], replicated, may hold values from 0.5 to 2
Outputs:
- fine_field: float32 [4, 32, 131072], P('sample', 'space')
- partner_field: float32 [4, 4, 2048], P('sample')
- coarse_field: float32 [32, 4, 2048], P(('space', 'sample'))
- estimate: float32 [2], replicated
Inputs may be any that keep to these rules, and one draw needn't show every extreme that they name: `plane_assign`: each row is a permutation of 0 to 17.
All inputs are finite; a program needn't handle non-finite values.
Results may differ from a plain program's by a relative error of at most 0.0003.
Values sent between devices are 32-bit elements; how exact they have to be, the bound alone decides.
A program may use at most 128 MiB of HBM per device.

v0:
```python
import math

import jax
import jax.numpy as jnp
from jax import lax
from jax.sharding import PartitionSpec as P

STEPS = 2


ADVECT = 0.3
DIFFUSE = 0.1
RELAX = 0.05
AMPLITUDE = 0.2
HIGHEST = lax.Precision.HIGHEST


def with_halo(cells, sides, width):
    for axis, dim in sides:
        count = lax.axis_size(axis)
        ends = count - 1
        head = lax.slice_in_dim(cells, 0, width, axis=dim)
        tail = lax.slice_in_dim(cells, cells.shape[dim] - width, cells.shape[dim], axis=dim)
        cells = jnp.concatenate(
            [
                lax.ppermute(tail, axis, [(i, (i + 1) % count) for i in range(ends)]),
                cells,
                lax.ppermute(head, axis, [((i + 1) % count, i) for i in range(ends)]),
            ],
            axis=dim,
        )
    return cells


def advance(extended, inflow, resistance):
    upstream = extended[..., :-2, :, :]
    centre = extended[..., 1:-1, :, :]
    downstream = extended[..., 2:, :, :]
    lateral = (
        jnp.roll(centre, 1, -2)
        + jnp.roll(centre, -1, -2)
        + jnp.roll(centre, 1, -1)
        + jnp.roll(centre, -1, -1)
        - 4.0 * centre
    )
    updated = (
        centre
        + ADVECT * (upstream - centre)
        + DIFFUSE * (upstream + downstream - 2.0 * centre)
        + DIFFUSE * lateral
        + RELAX * (inflow[..., None, :, :] - centre)
    )
    return updated / (1.0 + resistance)


def drag_field(
    turbine_x, turbine_y, turbine_z, thrust, first_plane, length, factor, y_count, z_count
):
    block_size = 8 // factor
    planes = first_plane + jnp.arange(length, dtype=jnp.int32)
    along_x = jnp.where(
        (turbine_x // factor)[:, None] == planes[None, :],
        thrust[:, None],
        jnp.zeros_like(thrust)[:, None],
    )
    y_index = jnp.arange(y_count, dtype=jnp.int32)
    z_index = jnp.arange(z_count, dtype=jnp.int32)
    low_y = (turbine_y * block_size)[:, None]
    low_z = (turbine_z * block_size)[:, None]
    cover_y = ((y_index[None, :] >= low_y) & (y_index[None, :] < low_y + 2 * block_size)).astype(
        thrust.dtype
    )
    cover_z = ((z_index[None, :] >= low_z) & (z_index[None, :] < low_z + 2 * block_size)).astype(
        thrust.dtype
    )
    cross_mask = (cover_y[:, :, None] * cover_z[:, None, :]).reshape(
        thrust.shape[0], y_count * z_count
    )
    return jnp.dot(along_x.T, cross_mask, precision=HIGHEST).reshape(length, y_count, z_count)


def restrict(values):
    leading = values.shape[:-2]
    y_count = values.shape[-2]
    z_count = values.shape[-1]
    return values.reshape(leading + (y_count // 8, 8, z_count // 8, 8)).mean(axis=(-3, -1))


def run_whole(velocity, inflow, resistance):
    for step_index in range(STEPS):
        extended = jnp.concatenate(
            [inflow[..., None, :, :], velocity, velocity[..., -1:, :, :]], axis=-3
        )
        velocity = advance(extended, inflow, resistance)
    return velocity


def twiddle(first_index, second_index, period):
    turn_count = first_index[:, None] * second_index[None, :] % period
    phases = 2.0 * math.pi / period * turn_count.astype(jnp.float32)
    return (jnp.cos(phases), jnp.sin(phases))


def shards(
    spectra,
    plane_assign,
    fine_state,
    partner_state,
    coarse_state,
    turbine_x,
    turbine_y,
    turbine_z,
    thrust,
):
    spaces = lax.axis_size("space")
    slab_index = lax.axis_index("space")
    ky_rows = spectra.shape[2]
    total_y = ky_rows * spaces
    total_z = spectra.shape[3]
    coarse_y = total_y // 8
    coarse_z = total_z // 8
    pair_count = fine_state.shape[0]
    slab_planes = fine_state.shape[1]
    norm_scale = 1.0 / math.sqrt(total_y * total_z)
    assignment = plane_assign[0]
    pair_spectra = jnp.take(spectra, assignment[:pair_count], axis=0)
    alone_spectra = jnp.take(spectra, assignment[pair_count:], axis=0)
    z_cells = jnp.arange(total_z, dtype=jnp.int32)
    y_cells = jnp.arange(total_y, dtype=jnp.int32)
    cosine_z, sine_z = twiddle(z_cells, z_cells, total_z)
    z_table = jnp.stack(
        [jnp.concatenate([cosine_z, sine_z], axis=1), jnp.concatenate([-sine_z, cosine_z], axis=1)]
    )
    cosine_y, sine_y = twiddle(y_cells, y_cells, total_y)
    y_table = jnp.stack([cosine_y, -sine_y])
    pair_pq = jnp.einsum("ncks,csj->nkj", pair_spectra, z_table, precision=HIGHEST).reshape(
        pair_count, ky_rows, 2, total_z
    )
    own_ky = slab_index * ky_rows + jnp.arange(ky_rows, dtype=jnp.int32)
    cosine_own, sine_own = twiddle(own_ky, y_cells, total_y)
    y_own = jnp.stack([cosine_own, -sine_own])
    partial_noise = jnp.einsum("nkcz,cky->nyz", pair_pq, y_own, precision=HIGHEST)
    fine_noise = lax.psum(partial_noise, "space") * norm_scale
    alone_pq = jnp.einsum("ncks,csj->nkj", alone_spectra, z_table, precision=HIGHEST)
    gathered_pq = lax.all_to_all(alone_pq, "space", split_axis=0, concat_axis=1, tiled=True)
    full_plane = jnp.einsum(
        "nkcz,cky->nyz", gathered_pq.reshape(-1, total_y, 2, total_z), y_table, precision=HIGHEST
    )
    alone_noise = restrict(full_plane * norm_scale)
    fine_inflow = 1.0 + AMPLITUDE * fine_noise
    last_plane = slab_planes * spaces - 1
    slab_start = slab_index * slab_planes
    velocity = fine_state.astype(jnp.float32).reshape(pair_count, slab_planes, total_y, total_z)
    fine_drag = drag_field(
        turbine_x, turbine_y, turbine_z, thrust, slab_start, slab_planes, 1, total_y, total_z
    )
    for step_index in range(STEPS):
        extended = with_halo(velocity, (("space", 1),), 1)
        start_plane = slab_start - 1
        length = extended.shape[1]
        global_x = start_plane + jnp.arange(length, dtype=jnp.int32)
        inside = jnp.clip(last_plane - start_plane, 0, length - 1)
        edge_plane = lax.dynamic_index_in_dim(extended, inside, axis=1, keepdims=True)
        below_mask = (global_x < 0)[None, :, None, None]
        above_mask = (global_x > last_plane)[None, :, None, None]
        velocity = advance(
            jnp.where(
                below_mask, fine_inflow[:, None], jnp.where(above_mask, edge_plane, extended)
            ),
            fine_inflow,
            fine_drag,
        )
    coarse_planes = slab_planes * spaces // 8
    coarse_drag = drag_field(
        turbine_x, turbine_y, turbine_z, thrust, 0, coarse_planes, 8, coarse_y, coarse_z
    )
    partner_inflow = 1.0 + AMPLITUDE * restrict(fine_noise)
    alone_inflow = 1.0 + AMPLITUDE * alone_noise
    partner = run_whole(
        partner_state.reshape(pair_count, coarse_planes, coarse_y, coarse_z),
        partner_inflow,
        coarse_drag,
    )
    alone_runs = run_whole(
        coarse_state.reshape(-1, coarse_planes, coarse_y, coarse_z), alone_inflow, coarse_drag
    )
    fine_power = jnp.sum(fine_drag * velocity * velocity * velocity, axis=(1, 2, 3)) / 256.0
    partner_power = jnp.sum(coarse_drag * partner * partner * partner, axis=(1, 2, 3)) / 4.0
    alone_power = jnp.sum(coarse_drag * alone_runs * alone_runs * alone_runs, axis=(1, 2, 3)) / 4.0
    leader = (slab_index == 0).astype(jnp.float32)
    partials = jnp.stack(
        [jnp.sum(fine_power) - leader * jnp.sum(partner_power), jnp.sum(alone_power)]
    )
    totals = lax.psum(partials, ("space", "sample"))
    samples_count = lax.axis_size("sample")
    counts = jnp.array(
        [pair_count * samples_count, alone_runs.shape[0] * spaces * samples_count], jnp.float32
    )
    estimate = totals / counts
    fine_field = velocity.reshape(pair_count, slab_planes, total_y * total_z)
    partner_field = partner.reshape(pair_count, coarse_planes, coarse_y * coarse_z)
    coarse_field = alone_runs.reshape(alone_runs.shape[0], coarse_planes, coarse_y * coarse_z)
    return (fine_field, partner_field, coarse_field, estimate)


def solution(mesh):
    placed = (
        P("sample", None, "space", None),
        P("sample", None),
        P("sample", "space", None),
        P("sample", None, None),
        P(("space", "sample"), None, None),
        P(),
        P(),
        P(),
        P(),
    )
    return jax.shard_map(
        shards,
        mesh=mesh,
        in_specs=placed,
        out_specs=(
            P("sample", "space", None),
            P("sample", None, None),
            P(("space", "sample"), None, None),
            P(),
        ),
        check_vma=False,
    )
```

profile of v0, /device:TPU:0, one launch (start us, length us, event | category | flops | bytes accessed | tf_op | source)
XLA Modules:
  0.0 247.3 jit_solution(2681329605193786550)
XLA Ops:
  7.2 1.0 fusion.114
  8.3 1.0 fusion.117
  11.6 0.8 copy-done.8
  12.4 0.8 fusion.42
  13.2 2.0 convolution_bitcast_fusion.1
  15.3 1.6 reshape.827
  16.9 1.5 fusion.172
  18.5 3.3 %collective-permute-start = (f32[2,1,512,256]{3,2,1,0:T(8,128)}, f32[2,1,512,256]{3,2,1,0:T(8,128)}, u32[]{:S(2)}, u32[]{:S(2)}) collective-permute-start(f32[2,1,512,256]{3,2,1,0:T(8,128)} %get-tuple-element.29), channel_id=1, source_target_pairs={{0,2},{2,4},{4,6},{6,8},{8,10},{10,12},{12,14},{14,16},{16,18},{18... | collective-permute-start | bytes 3145736 | tf_op jit(solution)/shard_map/ppermute | solution.py:26
  21.8 1.3 collective-permute-start.1
  23.2 1.6 gather_fusion.1
  24.8 4.4 %convolution_bitcast_fusion = f32[16,32,512]{2,1,0:T(8,128)} fusion(f32[16,2,32,256]{3,2,1,0:T(8,128)} %gather_fusion.1, f32[1,256,512]{2,1,0:T(8,128)} %copy-done.9, f32[1,256,512]{2,1,0:T(8,128)} %copy-done.8, pred[16]{0:T(512)(128)(4,1)S(1)} %compare_and_fusion), kind=kOutput, calls=%fused_computation.42 | convolution fusion | flops 1611137024 | bytes 3145744 | tf_op jit(solution)/shard_map/ncks,csj->nkj/dot_general | solution.py:144
  29.3 8.4 %all-to-all-start = ((f32[16,32,512]{2,1,0:T(8,128)}), f32[16,32,512]{2,1,0:T(8,128)}, u32[]{:S(2)}, u32[]{:S(2)}) async-start(f32[16,32,512]{2,1,0:T(8,128)} %convolution_bitcast_fusion), calls=%async_computation | async-start | bytes 2097152 | tf_op jit(solution)/shard_map/all_to_all | solution.py:145
  37.8 0.8 fusion.179
  38.6 0.9 fusion.177
  39.5 0.9 fusion.178
  41.5 0.8 reshape.824
  42.3 5.0 %sine_negate_fusion = (f32[1,512,512]{1,2,0:T(8,128)}, f32[1,512,512]{1,2,0:T(8,128)}) fusion(), kind=kLoop, calls=%fused_computation.52 | loop fusion | flops 3932160 | bytes 2097152 | tf_op jit(solution)/shard_map/neg | solution.py:135
  47.4 0.8 fusion.187
  48.2 0.7 fusion.185
  48.9 0.7 fusion.186
  51.0 1.2 broadcast_multiply_fusion
  52.2 7.8 %fusion = f32[2,512,256]{2,0,1:T(2,128)S(1)} fusion(f32[16]{0:T(128)S(1)} %copy-done.17, s32[16]{0:T(128)S(1)} %copy-done.22, s32[2]{0:T(128)S(1)} %iota_add_fusion, f32[2,8,512,256]{3,2,1,0:T(8,128)S(1)} %bitcast.72), kind=kOutput, calls=%fused_computation.2 | convolution fusion | flops 50331712 | bytes 9437320 | tf_op jit(solution)/shard_map/dot_general | solution.py:79
  60.1 1.5 broadcast_add_fusion
  61.6 61.0 %all-reduce.2.cloned.1.call-done = f32[2,512,256]{2,1,0:T(8,128)} async-done(((f32[2,512,256]{2,1,0:T(8,128)}), f32[2,512,256]{2,1,0:T(8,128)}) %all-reduce.2.cloned.1.call-update) | async-done | bytes 1048592 | tf_op jit(solution)/shard_map/psum | solution.py:143
  122.6 2.4 broadcast_multiply_fusion.1
  125.0 12.1 %reshape.818 = f32[2,64,8,32,8]{4,3,2,1,0:T(8,128)} reshape(f32[2,512,256]{2,1,0:T(8,128)} %get-tuple-element.30) | data formatting | bytes 2097152 | tf_op jit(solution)/shard_map/reshape | solution.py:86
  137.1 7.0 %reduce_sum.67 = f32[2,64,32]{2,1,0:T(8,128)S(1)} reduce(f32[2,64,8,32,8]{4,3,2,1,0:T(8,128)} %reshape.818, f32[]{:T(128)} %constant.168.clone.1), dimensions={2,4}, to_apply=%region_1.2 | reduce | flops 258048 | bytes 1064964 | tf_op jit(solution)/shard_map/reduce_sum | solution.py:86
  144.1 1.7 fusion.66
  147.3 0.8 reshape.820
  149.3 1.3 constant_dynamic-update-slice_fusion.2
  150.8 1.3 constant_dynamic-update-slice_fusion
  154.8 2.8 %fusion.15 = f32[2,2,512,256]{3,2,1,0:T(8,128)S(1)} fusion(f32[2,4,512,256]{3,2,1,0:T(8,128)S(1)} %select_select_fusion.1, f32[2,2,511,256]{3,2,1,0:T(8,128)S(1)} %get-tuple-element.23, f32[2,2,1,256]{3,2,1,0:T(1,128)S(1)} %get-tuple-element.25, f32[2,2,1,256]{3,2,1,0:T(1,128)S(1)} %get-tuple-element.24, f32[2,2,511,256]{3,2,1,0:T(8,128)S(1)} %get-tuple-element.22, ...), kind=kLoop, calls=%fused_computation.24 | loop fusion | flops 12058624 | bytes 18874368 | tf_op jit(solution)/shard_map/div | solution.py:53
  157.6 1.5 fusion.171
  159.1 1.3 collective-permute-start.3
  160.4 4.0 %collective-permute-start.2 = (f32[2,1,512,256]{3,2,1,0:T(8,128)}, f32[2,1,512,256]{3,2,1,0:T(8,128)}, u32[]{:S(2)}, u32[]{:S(2)}) collective-permute-start(f32[2,1,512,256]{3,2,1,0:T(8,128)} %get-tuple-element.26), channel_id=1, source_target_pairs={{0,2},{2,4},{4,6},{6,8},{8,10},{10,12},{12,14},{14,16},{16,18},{18... | collective-permute-start | bytes 3145736 | tf_op jit(solution)/shard_map/ppermute | solution.py:26
  164.4 2.9 %reshape.822 = f32[512,2,256]{2,1,0:T(2,128)} reshape(f32[16,32,512]{2,1,0:T(8,128)} %all-to-all-done) | data formatting | bytes 2097152 | tf_op jit(solution)/shard_map/reshape.7
  167.3 4.5 %fusion.31 = f32[512,256]{1,0:T(8,128)} fusion(f32[1,512,512]{1,2,0:T(8,128)} %get-tuple-element.84, f32[1,512,512]{1,2,0:T(8,128)} %get-tuple-element.85, f32[512,2,256]{2,1,0:T(2,128)} %reshape.822), kind=kOutput, calls=%fused_computation.45 | convolution fusion | flops 1611268096 | bytes 3670016 | tf_op jit(solution)/shard_map/nkcz,cky->nyz/dot_general | solution.py:146
  171.8 7.1 %reshape.823 = f32[64,8,32,8]{3,2,1,0:T(8,128)} reshape(f32[512,256]{1,0:T(8,128)} %fusion.31) | data formatting | bytes 1048576 | tf_op jit(solution)/shard_map/reshape | solution.py:86
  178.9 4.1 %reduce_sum.68 = f32[64,32]{1,0:T(8,128)S(1)} reduce(f32[64,8,32,8]{3,2,1,0:T(8,128)} %reshape.823, f32[]{:T(128)} %constant.168.clone.1), dimensions={1,3}, to_apply=%region_2.3 | reduce | flops 129024 | bytes 532484 | tf_op jit(solution)/shard_map/reduce_sum | solution.py:86
  183.0 1.4 fusion.100
  184.6 0.8 fusion.81
  185.4 0.7 reshape.825
  186.8 2.0 pad_maximum_fusion
  188.9 2.1 select_select_fusion
  192.5 0.8 copy-done.5
  193.7 3.2 %fusion.3 = (f32[2]{0:T(128)S(1)}, f32[2,2,512,256]{3,2,1,0:T(8,128)S(1)}) fusion(f32[2,512,256]{2,1,0:T(8,128)S(1)} %copy-done.10, f32[2,512,256]{2,1,0:T(8,128)S(1)} %copy-done.5, f32[2,512,256]{2,1,0:T(8,128)S(1)} %get-tuple-element.31, f32[2,2,512,1]{3,2,1,0:T(8,128)S(1)} %get-tuple-element.15, f32[2,2,512,255]{3,2,1,0:T(8,128)S(1)} %get-tuple-element.17, ...), kind=kLoop, calls=%fused_computation.10 | loop fusion | flops 14155774 | bytes 19922952 | tf_op jit(solution)/shard_map/reduce_sum | solution.py:187
  198.2 2.4 reshape.816
  200.6 39.4 %psum.15 = f32[2]{0:T(128)S(1)} all-reduce(f32[2]{0:T(128)S(1)} %pad_maximum_fusion.9), channel_id=1, replica_groups=mesh['space'=16,'sample'=2] {'space','sample'}, use_global_device_ids=true, to_apply=%region_8.9 | all-reduce | flops 2 | bytes 16 | tf_op jit(solution)/shard_map/psum | solution.py:194
  (116 shorter events, 13.3 us)
Async XLA Ops:
  7.2 3.8 %copy-start = (f32[18,2,32,256]{3,2,1,0:T(8,128)S(1)}, f32[18,2,32,256]{3,2,1,0:T(8,128)}, u32[]{:S(2)}) copy-start(f32[18,2,32,256]{3,2,1,0:T(8,128)} %param.10) | copy-start | bytes 3538948
  7.2 115.4 %all-reduce.2.cloned.1.call-start = ((), (), s32[]{:S(2)}) async-start(), calls=%async_computation.1 | async-start | bytes 2097152 | tf_op jit(solution)/shard_map/psum | solution.py:143
  11.6 0.8 copy-start.8
  11.6 1.6 copy-start.9
  16.9 6.2 %copy-start.23 = (s32[1,18]{1,0:T(1,128)S(1)}, s32[1,18]{1,0:T(1,128)}, u32[]{:S(2)}) copy-start(s32[1,18]{1,0:T(1,128)} %param.11) | copy-start | bytes 220
  18.5 130.8 %collective-permute-start = (f32[2,1,512,256]{3,2,1,0:T(8,128)}, f32[2,1,512,256]{3,2,1,0:T(8,128)}, u32[]{:S(2)}, u32[]{:S(2)}) collective-permute-start(f32[2,1,512,256]{3,2,1,0:T(8,128)} %get-tuple-element.29), channel_id=1, source_target_pairs={{0,2},{2,4},{4,6},{6,8},{8,10},{10,12},{12,14},{14,16},{16,18},{18... | collective-permute-start | bytes 3145736 | tf_op jit(solution)/shard_map/ppermute | solution.py:26
  21.8 129.0 %collective-permute-start.1 = (f32[2,1,512,256]{3,2,1,0:T(8,128)}, f32[2,1,512,256]{3,2,1,0:T(8,128)}, u32[]{:S(2)}, u32[]{:S(2)}) collective-permute-start(f32[2,1,512,256]{3,2,1,0:T(8,128)} %get-tuple-element.28), channel_id=1, source_target_pairs={{2,0},{4,2},{6,4},{8,6},{10,8},{12,10},{14,12},{16,14},{18,16},{20... | collective-permute-start | bytes 3145736 | tf_op jit(solution)/shard_map/ppermute | solution.py:28
  24.8 12.8 %copy-start.15 = (f32[2,4,2048]{2,1,0:T(4,128)S(1)}, f32[2,4,2048]{2,1,0:T(4,128)}, u32[]{:S(2)}) copy-start(f32[2,4,2048]{2,1,0:T(4,128)} %param.13) | copy-start | bytes 196612
  29.3 135.2 %all-to-all-start = ((f32[16,32,512]{2,1,0:T(8,128)}), f32[16,32,512]{2,1,0:T(8,128)}, u32[]{:S(2)}, u32[]{:S(2)}) async-start(f32[16,32,512]{2,1,0:T(8,128)} %convolution_bitcast_fusion), calls=%async_computation | async-start | bytes 2097152 | tf_op jit(solution)/shard_map/all_to_all | solution.py:145
  37.6 2.8 %copy-start.20 = (s32[16]{0:T(128)S(1)}, s32[16]{0:T(128)}, u32[]{:S(2)}) copy-start(s32[16]{0:T(128)} %param.17) | copy-start | bytes 196
  37.6 2.8 %copy-start.21 = (s32[16]{0:T(128)S(1)}, s32[16]{0:T(128)}, u32[]{:S(2)}) copy-start(s32[16]{0:T(128)} %param.16) | copy-start | bytes 196
  37.8 3.2 %copy-start.2 = (f32[2,4,64,32]{3,2,1,0:T(8,128)}, f32[2,4,64,32]{3,2,1,0:T(8,128)S(1)}, u32[]{:S(2)}) copy-start(f32[2,4,64,32]{3,2,1,0:T(8,128)S(1)} %reshape.817) | copy-start | bytes 196612
  37.8 3.2 %copy-start.22 = (s32[16]{0:T(128)S(1)}, s32[16]{0:T(128)}, u32[]{:S(2)}) copy-start(s32[16]{0:T(128)} %param.15) | copy-start | bytes 196
  37.8 3.3 %copy-start.17 = (f32[16]{0:T(128)S(1)}, f32[16]{0:T(128)}, u32[]{:S(2)}) copy-start(f32[16]{0:T(128)} %param.18) | copy-start | bytes 196
  40.4 6.9 %copy-start.16 = (f32[1,4,2048]{2,1,0:T(4,128)S(1)}, f32[1,4,2048]{2,1,0:T(4,128)}, u32[]{:S(2)}) copy-start(f32[1,4,2048]{2,1,0:T(4,128)} %param.14) | copy-start | bytes 98308
  41.5 9.3 %copy-start.13 = (f32[4,64,32]{2,1,0:T(8,128)}, f32[4,64,32]{2,1,0:T(8,128)S(1)}, u32[]{:S(2)}) copy-start(f32[4,64,32]{2,1,0:T(8,128)S(1)} %reshape.819) | copy-start | bytes 98308
  47.4 12.7 %copy-start.6 = (f32[1,4,64,32]{3,2,1,0:T(8,128)}, f32[1,4,64,32]{3,2,1,0:T(8,128)S(1)}, u32[]{:S(2)}) copy-start(f32[1,4,64,32]{3,2,1,0:T(8,128)S(1)} %reshape.821) | copy-start | bytes 98308
  137.0 7.1 %copy-start.3 = (f32[2,4,64,32]{3,2,1,0:T(8,128)S(1)}, f32[2,4,64,32]{3,2,1,0:T(8,128)}, u32[]{:S(2)}) copy-start(f32[2,4,64,32]{3,2,1,0:T(8,128)} %copy-done.2) | copy-start | bytes 196612
  137.0 7.1 %slice-start = ((f32[2,4,64,32]{3,2,1,0:T(8,128)}), f32[2,1,64,32]{3,2,1,0:T(8,128)S(1)}, s32[]{:S(2)}) async-start(f32[2,4,64,32]{3,2,1,0:T(8,128)} %copy-done.2), calls=%async_computation.2 | async-start | bytes 131072 | tf_op jit(solution)/shard_map/slice | solution.py:92
  145.8 0.9 copy-start.12
  145.9 1.0 copy-start.14
  150.8 1.4 copy-start.18
  150.8 1.4 copy-start.19
  153.6 1.2 copy-start.4
  159.1 27.7 %collective-permute-start.3 = (f32[2,1,512,256]{3,2,1,0:T(8,128)}, f32[2,1,512,256]{3,2,1,0:T(8,128)}, u32[]{:S(2)}, u32[]{:S(2)}) collective-permute-start(f32[2,1,512,256]{3,2,1,0:T(8,128)} %get-tuple-element.27), channel_id=1, source_target_pairs={{2,0},{4,2},{6,4},{8,6},{10,8},{12,10},{14,12},{16,14},{18,16},{20... | collective-permute-start | bytes 3145736 | tf_op jit(solution)/shard_map/ppermute | solution.py:28
  160.4 26.4 %collective-permute-start.2 = (f32[2,1,512,256]{3,2,1,0:T(8,128)}, f32[2,1,512,256]{3,2,1,0:T(8,128)}, u32[]{:S(2)}, u32[]{:S(2)}) collective-permute-start(f32[2,1,512,256]{3,2,1,0:T(8,128)} %get-tuple-element.26), channel_id=1, source_target_pairs={{0,2},{2,4},{4,6},{6,8},{8,10},{10,12},{12,14},{14,16},{16,18},{18... | collective-permute-start | bytes 3145736 | tf_op jit(solution)/shard_map/ppermute | solution.py:26
  178.8 4.1 %copy-start.7 = (f32[1,4,64,32]{3,2,1,0:T(8,128)S(1)}, f32[1,4,64,32]{3,2,1,0:T(8,128)}, u32[]{:S(2)}) copy-start(f32[1,4,64,32]{3,2,1,0:T(8,128)} %copy-done.6) | copy-start | bytes 98308
  178.8 4.1 %slice-start.1 = ((f32[1,4,64,32]{3,2,1,0:T(8,128)}), f32[1,1,64,32]{3,2,1,0:T(8,128)S(1)}, s32[]{:S(2)}) async-start(f32[1,4,64,32]{3,2,1,0:T(8,128)} %copy-done.6), calls=%async_computation.3 | async-start | bytes 65536 | tf_op jit(solution)/shard_map/slice | solution.py:92
  178.9 4.1 %copy-start.11 = (f32[1,4,64,32]{3,2,1,0:T(8,128)S(1)}, f32[1,4,64,32]{3,2,1,0:T(8,128)}, u32[]{:S(2)}) copy-start(f32[1,4,64,32]{3,2,1,0:T(8,128)} %reshape.824) | copy-start | bytes 98308
  192.1 1.2 copy-start.5
  192.1 1.5 copy-start.10
  198.2 42.3 %copy-start.1 = (f32[18,2,32,256]{3,2,1,0:T(8,128)S(1)}, f32[18,2,32,256]{3,2,1,0:T(8,128)}, u32[]{:S(2)}) copy-start(f32[18,2,32,256]{3,2,1,0:T(8,128)} %param.10) | copy-start | bytes 3538948
  198.2 41.8 %copy-start.24 = (f32[2]{0:T(128)S(1)}, f32[2]{0:T(128)}, u32[]{:S(2)}) copy-start(f32[2]{0:T(128)} %constant.181) | copy-start | bytes 28
Sparse Core Ops, SparseCore 0:
  15.4 107.1 all-reduce.1
where the time goes:
time: 248 us; the launch traced here: 247 us
  waiting for transfers between devices  61 us (25%)
  local copies, waits for them, and re-layouts  48.3 us (19%)
  other arithmetic  43.8 us (18%)
  blocking collectives  39.4 us (16%)
  matrix products  19.8 us (8%)
  starting transfers between devices  18.3 us (7%)
  between operations  16.6 us (7%)
    psum x1, waiting for transfers between devices, shards(): fine_noise = lax.psum(partial_noise, 'space') * norm_scale  61 us
    psum x1, blocking collectives, shards(): totals = lax.psum(partials, ('space', 'sample'))  39.4 us
    reshape x2, local copies, waits for them, and re-layouts, restrict(): values.reshape(leading + (y_count // 8, 8, z_count // 8, 8))  19.2 us
    reduce_sum x2, other arithmetic, restrict(): values.reshape(leading + (y_count // 8, 8, z_count // 8, 8))  11.1 us
    all_to_all x1, starting transfers between devices, shards(): lax.all_to_all(alone_pq, 'space', split_axis=0, concat_axis=1, tiled=True)  8.37 us
    dot_general x2, matrix products, drag_field(): jnp.dot(along_x.T, cross_mask, precision=HIGHEST)  8.14 us
    ppermute x2, starting transfers between devices, with_halo(): lax.ppermute(tail, axis, [(i, (i + 1) % count) for i in range(ends)])  7.36 us
    div x3, other arithmetic, advance(): return updated / (1.0 + resistance)  5.88 us
  transfers between devices with their start and end apart: 6, of which 1 were waited for; matrix products, arithmetic and copies ran while one was open for 36% of the time, Pallas kernels for 0%

commit v1 on v0

v1 whole, which is shorter than its diff:
```python
import functools
import math

import jax
import jax.numpy as jnp
import ml_dtypes
import numpy as np
from jax import lax
from jax.experimental import pallas as pl
from jax.experimental.pallas import tpu as pltpu
from jax.sharding import PartitionSpec as P

AMPLITUDE = 0.2
HIGHEST = lax.Precision.HIGHEST
MESH = pl.DeviceIdType.MESH
F32 = jnp.float32
BF16 = jnp.bfloat16
NT = (((1,), (1,)), ((), ()))


def halves(table):
    high = table.astype(np.float32).astype(ml_dtypes.bfloat16)
    low = (table - high.astype(np.float64)).astype(np.float32).astype(ml_dtypes.bfloat16)
    return np.stack([high, low])


def tables(spaces, ky_rows, total_z):
    total_y = spaces * ky_rows
    z = np.arange(total_z)
    phase_z = 2 * np.pi / total_z * (np.outer(z, z) % total_z)
    cz, sz = np.cos(phase_z), np.sin(phase_z)
    z_table = np.block([[cz, sz], [-sz, cz]])
    y = np.arange(total_y)
    phase_y = 2 * np.pi / total_y * (np.outer(y, y) % total_y)
    cy, sy = np.cos(phase_y), np.sin(phase_y)
    order = y.reshape(spaces // 2, 2, ky_rows).transpose(1, 0, 2).reshape(-1)
    y_table = np.concatenate([cy[:, order], -sy[:, order]], axis=1)
    z_small = z_table.reshape(2 * total_z, 2, total_z // 8, 8).mean(-1).reshape(2 * total_z, -1)
    y_small = np.concatenate(
        [cy.reshape(total_y // 8, 8, total_y).mean(1), -sy.reshape(total_y // 8, 8, total_y).mean(1)]
    )
    return halves(z_table), halves(y_table), halves(z_small), halves(y_small)


def split(x):
    high = x.astype(BF16)
    return high, (x - high.astype(F32)).astype(BF16)


def dot(a, b):
    return jnp.dot(a, b, preferred_element_type=F32)


def dot_right(x, high, low):
    xh, xl = split(x)
    return dot(xh, high) + dot(xl, high) + dot(xh, low)


def dot_left(high, low, x):
    xh, xl = split(x)
    return dot(high, xh) + dot(high, xl) + dot(low, xh)


def kernel(
    spaces, samples, coarse_planes,
    fine_hbm, spec, assign, partner, coarse, turbines, thrust, zt_hbm, yt_hbm, z_small, y_small,
    rep, fine_out, partner_out, coarse_out, est_out,
    own, halo, block, gath, al_in, al_out, al_recv, zt, yt, pq_hi, pq_lo, g_ref, rk, kd, u1, part,
    parts, group, groups,
    halo_s, halo_r, own_sem, zt_sem, yt_sem, gx_s, gz_s, gc_s, g_r, gc_r, al_s, al_r, p_s, p_r,
    q_s, q_r,
):
    me = lax.axis_index("space")
    sample = lax.axis_index("sample")
    last = spaces - 1
    pairs, _, ny, nz = fine_hbm.shape
    ky = spec.shape[2]
    yc, width = coarse.shape[1], coarse.shape[2]
    zc = width // coarse_planes
    core = lax.rem(me, 2)
    chip = me // 2
    across = lax.rem(chip, 2)
    level = chip // 2
    levels = spaces // 4
    chip_x = chip + 1 - 2 * across
    dev_x = chip_x * 2 + core
    dev_c = me + 1 - 2 * core

    def remote(src, dst, send, recv, **where):
        return pltpu.make_async_remote_copy(
            src_ref=src, dst_ref=dst, send_sem=send, recv_sem=recv, device_id=where,
            device_id_type=MESH,
        )

    def others(count, mine, body):
        def step(i, carry):
            @pl.when(i != mine)
            def _():
                body(i)

            return carry

        lax.fori_loop(0, count, step, 0)

    barrier = pltpu.get_barrier_semaphore()
    others(spaces, me, lambda i: pl.semaphore_signal(
        barrier, inc=1, device_id={"space": i}, device_id_type=MESH))
    others(samples, sample, lambda i: pl.semaphore_signal(
        barrier, inc=1, device_id={"sample": i}, device_id_type=MESH))
    pl.semaphore_wait(barrier, spaces + samples - 2)

    def to_right(n, p):
        return remote(fine_hbm.at[n, p], halo.at[0, n, p], halo_s.at[0, n, p], halo_r.at[0, n, p],
                      space=jnp.minimum(me + 1, last))

    def to_left(n, p):
        return remote(fine_hbm.at[n, p], halo.at[1, n, p], halo_s.at[1, n, p], halo_r.at[1, n, p],
                      space=jnp.maximum(me - 1, 0))

    @pl.when(me < last)
    def _():
        for n in range(pairs):
            for p in (1, 0):
                to_right(n, p).start()

    @pl.when(me > 0)
    def _():
        for n in range(pairs):
            for p in (0, 1):
                to_left(n, p).start()

    zt_copy = pltpu.make_async_copy(zt_hbm, zt, zt_sem)
    yt_copy = pltpu.make_async_copy(yt_hbm, yt, yt_sem)
    own_copy = pltpu.make_async_copy(fine_hbm, own, own_sem)
    zt_copy.start()
    yt_copy.start()
    own_copy.start()

    for n in range(pairs):
        planes = spec[assign[0, n]]
        block[2 * n : 2 * n + 2] = planes
        gath[core, chip, 2 * n : 2 * n + 2] = planes

    def stage(p, carry):
        planes = spec[assign[0, pairs + p]]
        rows = pl.ds(pl.multiple_of(p * ky, ky), ky)
        al_in[rows, 0:nz] = planes[0]
        al_in[rows, nz : 2 * nz] = planes[1]
        return carry

    lax.fori_loop(0, spaces, stage, 0)

    send_x = remote(block, gath.at[core, chip], gx_s, g_r.at[chip], space=dev_x)
    send_x.start()

    def along(k, which, src, chip_of):
        return remote(src, gath.at[core, chip_of], gz_s.at[which, k], g_r.at[chip_of],
                      space=(k * 2 + across) * 2 + core)

    others(levels, level, lambda k: along(k, 0, block, chip).start())

    z_out = dot_right(al_in[...], z_small[0], z_small[1])
    al_out[...] = z_out.reshape(spaces, ky, 2 * zc)
    al_recv[me] = al_out[me]

    tx, ty, tz = turbines[0:1], turbines[1:2], turbines[2:3]
    count = tx.shape[1]

    def cover(index, low, size):
        return jnp.where((index >= low) & (index < low + 2 * size), 1.0, 0.0).astype(F32)

    cover_y = cover(lax.broadcasted_iota(jnp.int32, (ny, count), 0), ty * 8, 8)
    cover_z = cover(lax.broadcasted_iota(jnp.int32, (nz, count), 0), tz * 8, 8)

    for j in range(4):
        weight = jnp.where(tx == me * 2 + (j - 1), thrust[...], 0.0)
        drag = lax.dot_general(cover_y, cover_z * weight, NT, precision=HIGHEST,
                               preferred_element_type=F32)
        if j in (1, 2):
            kd[j - 1] = drag
        rk[j] = 1.0 / (1.0 + drag)

    def send_alone(p):
        return remote(al_out.at[p], al_recv.at[me], al_s.at[p], al_r.at[me], space=p)

    others(spaces, me, lambda p: send_alone(p).start())

    cell = lax.broadcasted_iota(jnp.int32, (width, count), 0)
    weight_c = jnp.where(tx // 8 == cell // zc, thrust[...], 0.0)
    cover_zc = cover(cell % zc, tz, 1)
    cover_yc = cover(lax.broadcasted_iota(jnp.int32, (yc, count), 0), ty, 1)
    kc = lax.dot_general(cover_yc, cover_zc * weight_c, NT, precision=HIGHEST,
                         preferred_element_type=F32)
    rkc = 1.0 / (1.0 + kc)

    def got(c):
        remote(block, gath.at[core, c], gx_s, g_r.at[c], space=dev_x).wait_recv()

    got(chip_x)
    others(levels, level, lambda k: along(k, 1, gath.at[core, chip_x], chip_x).start())
    others(levels, level, lambda k: got(k * 2 + across))
    others(levels, level, lambda k: got(k * 2 + 1 - across))
    send_c = remote(gath.at[core], gath.at[core], gc_s, gc_r, space=dev_c)
    send_c.start()

    others(spaces, me, lambda p: remote(
        al_out.at[p], al_recv.at[p], al_s.at[p], al_r.at[p], space=p).wait_recv())
    norm = 1.0 / math.sqrt(ny * nz)
    folded = dot_left(y_small[0], y_small[1], al_recv[...].reshape(spaces * ky, 2 * zc))
    alone = jnp.dot(folded[0:yc], rep[0], precision=HIGHEST, preferred_element_type=F32) + jnp.dot(
        folded[yc : 2 * yc], rep[1], precision=HIGHEST, preferred_element_type=F32)
    alone_g = 1.0 + (AMPLITUDE * norm) * alone

    lane = lax.broadcasted_iota(jnp.int32, (yc, width), 1)
    z_at = lane % zc

    def coarse_run(u, g):
        for _ in range(2):
            west = jnp.where(z_at == 0, pltpu.roll(u, width - zc + 1, 1), pltpu.roll(u, 1, 1))
            east = jnp.where(z_at == zc - 1, pltpu.roll(u, zc - 1, 1), pltpu.roll(u, width - 1, 1))
            up = jnp.where(lane < zc, g, pltpu.roll(u, zc, 1))
            down = jnp.where(lane >= width - zc, u, pltpu.roll(u, width - zc, 1))
            side = west + east + pltpu.roll(u, 1, 0) + pltpu.roll(u, yc - 1, 0)
            u = (0.05 * (u + g) + 0.4 * up + 0.1 * (down + side)) * rkc
        return u

    run = coarse_run(coarse[0], alone_g)
    coarse_out[0] = run
    alone_power = jnp.sum(kc * run * run * run) * 0.25

    zt_copy.wait()
    yt_copy.wait()
    send_c.wait_recv()
    rows = 128

    def z_stage(n, carry):
        real = gath[:, :, 2 * n].reshape(ny, nz)
        imag = gath[:, :, 2 * n + 1].reshape(ny, nz)
        pq = dot_right(jnp.concatenate([real, imag], axis=1), zt[0], zt[1])
        high, low = split(pq)
        for c in range(2):
            pq_hi[n, c * ny : (c + 1) * ny] = high[:, c * nz : (c + 1) * nz]
            pq_lo[n, c * ny : (c + 1) * ny] = low[:, c * nz : (c + 1) * nz]
        return carry

    lax.fori_loop(0, pairs, z_stage, 0)

    def y_stage(i, carry):
        n, r = i // (ny // rows), lax.rem(i, ny // rows)
        at = pl.ds(pl.multiple_of(r * rows, rows), rows)
        noise = (dot(yt[0, at], pq_hi[n]) + dot(yt[0, at], pq_lo[n]) + dot(yt[1, at], pq_hi[n]))
        g_ref[n, at] = 1.0 + (AMPLITUDE * norm) * noise
        return carry

    lax.fori_loop(0, pairs * (ny // rows), y_stage, 0)

    mean_z = jnp.where(
        lax.broadcasted_iota(jnp.int32, (nz, width), 0) // 8
        == lax.broadcasted_iota(jnp.int32, (nz, width), 1) % zc, 0.125, 0.0).astype(BF16)
    mean_y = jnp.where(
        lax.broadcasted_iota(jnp.int32, (yc, ny), 1) // 8
        == lax.broadcasted_iota(jnp.int32, (yc, ny), 0), 0.125, 0.0).astype(BF16)
    partner_power = 0.0
    for n in range(pairs):
        gh, gl = split(g_ref[n] - 1.0)
        th, tl = split(dot(gh, mean_z) + dot(gl, mean_z))
        partner_g = 1.0 + dot(mean_y, th) + dot(mean_y, tl)
        run = coarse_run(partner[n], partner_g)
        partner_out[n] = run
        partner_power += jnp.sum(kc * run * run * run) * 0.25

    own_copy.wait()

    def advance(c, w, e, g, r):
        side = pltpu.roll(c, 1, 0) + pltpu.roll(c, ny - 1, 0) + pltpu.roll(c, 1, 1) + pltpu.roll(
            c, nz - 1, 1)
        return (0.05 * (c + g) + 0.4 * w + 0.1 * (e + side)) * r

    def fine(n, power):
        g = g_ref[n]

        @pl.when(me > 0)
        def _():
            for p in (1, 0):
                to_right(n, p).wait_recv()
            u1[0] = advance(halo[0, n, 1], halo[0, n, 0], own[n, 0], g, rk[0])

        @pl.when(me == 0)
        def _():
            halo[0, n, 1] = g
            u1[0] = g

        @pl.when(me < last)
        def _():
            for p in (0, 1):
                to_left(n, p).wait_recv()
            u1[3] = advance(halo[1, n, 0], own[n, 1], halo[1, n, 1], g, rk[3])

        @pl.when(me == last)
        def _():
            halo[1, n, 0] = own[n, 1]

        u1[1] = advance(own[n, 0], halo[0, n, 1], own[n, 1], g, rk[1])
        u1[2] = advance(own[n, 1], own[n, 0], halo[1, n, 0], g, rk[2])

        @pl.when(me == last)
        def _():
            u1[3] = u1[2]

        for p in range(2):
            u = advance(u1[1 + p], u1[p], u1[2 + p], g, rk[1 + p])
            fine_out[n, p] = u
            power += jnp.sum(kd[p] * u * u * u)
        return power

    fine_power = lax.fori_loop(0, pairs, fine, jnp.float32(0.0)) * (1.0 / 256.0)
    leader = jnp.where(me == 0, 1.0, 0.0)
    lane8 = lax.broadcasted_iota(jnp.int32, (8, 128), 1)
    part[...] = jnp.where(lane8 == 0, fine_power - leader * partner_power,
                          jnp.where(lane8 == 1, alone_power, 0.0))
    parts[me] = part[...]

    def send_part(p):
        return remote(part, parts.at[me], p_s.at[p], p_r.at[me], space=p)

    others(spaces, me, lambda p: send_part(p).start())
    others(spaces, me, lambda p: remote(
        part, parts.at[p], p_s.at[p], p_r.at[p], space=p).wait_recv())
    group[...] = jnp.sum(parts[...], axis=0)
    groups[sample] = group[...]
    others(samples, sample, lambda p: remote(
        group, groups.at[sample], q_s.at[p], q_r.at[sample], sample=p).start())
    others(samples, sample, lambda p: remote(
        group, groups.at[p], q_s.at[p], q_r.at[p], sample=p).wait_recv())
    total = jnp.sum(groups[...], axis=0)
    est_out[...] = jnp.where(lane8 == 0, total * (1.0 / (pairs * samples)),
                             total * (1.0 / (spaces * samples)))

    @pl.when(me < last)
    def _():
        for n in range(pairs):
            for p in (1, 0):
                to_right(n, p).wait_send()

    @pl.when(me > 0)
    def _():
        for n in range(pairs):
            for p in (0, 1):
                to_left(n, p).wait_send()

    send_x.wait_send()
    others(levels, level, lambda k: along(k, 0, block, chip).wait_send())
    others(levels, level, lambda k: along(k, 1, gath.at[core, chip_x], chip_x).wait_send())
    send_c.wait_send()
    others(spaces, me, lambda p: send_alone(p).wait_send())
    others(spaces, me, lambda p: send_part(p).wait_send())
    others(samples, sample, lambda p: remote(
        group, groups.at[sample], q_s.at[p], q_r.at[sample], sample=p).wait_send())


def shards(
    spaces, samples, spectra, plane_assign, fine_state, partner_state, coarse_state,
    turbine_x, turbine_y, turbine_z, thrust,
):
    ky, nz = spectra.shape[2:]
    ny = ky * spaces
    pairs, slab = fine_state.shape[:2]
    planes = partner_state.shape[1]
    yc, zc = ny // 8, nz // 8
    width = planes * zc
    levels = spaces // 4
    zt, yt, zs, ys = tables(spaces, ky, nz)
    rep = np.zeros((2, 2 * zc, width), np.float32)
    for c in range(2):
        for x in range(planes):
            rep[c, c * zc + np.arange(zc), x * zc + np.arange(zc)] = 1.0

    def pack(state):
        return state.reshape(-1, planes, yc, zc).transpose(0, 2, 1, 3).reshape(-1, yc, width)

    def unpack(state):
        return state.reshape(-1, yc, planes, zc).transpose(0, 2, 1, 3).reshape(-1, planes, yc * zc)

    vmem = pl.BlockSpec(memory_space=pltpu.VMEM)
    anywhere = pl.BlockSpec(memory_space=pl.ANY)
    dma = pltpu.SemaphoreType.DMA
    field, partner, alone, est = pl.pallas_call(
        functools.partial(kernel, spaces, samples, planes),
        out_shape=(
            jax.ShapeDtypeStruct((pairs, slab, ny, nz), F32),
            jax.ShapeDtypeStruct((pairs, yc, width), F32),
            jax.ShapeDtypeStruct((1, yc, width), F32),
            jax.ShapeDtypeStruct((8, 128), F32),
        ),
        in_specs=[anywhere, vmem, pl.BlockSpec(memory_space=pltpu.SMEM), vmem, vmem, vmem, vmem,
                  anywhere, anywhere, vmem, vmem, vmem],
        out_specs=(vmem,) * 4,
        scratch_shapes=[
            pltpu.VMEM((pairs, 2, ny, nz), F32),
            pltpu.VMEM((2, pairs, 2, ny, nz), F32),
            pltpu.VMEM((2 * pairs, ky, nz), F32),
            pltpu.VMEM((2, spaces // 2, 2 * pairs, ky, nz), F32),
            pltpu.VMEM((spaces * ky, 2 * nz), F32),
            pltpu.VMEM((spaces, ky, 2 * zc), F32),
            pltpu.VMEM((spaces, ky, 2 * zc), F32),
            pltpu.VMEM(zt.shape, BF16),
            pltpu.VMEM(yt.shape, BF16),
            pltpu.VMEM((pairs, 2 * ny, nz), BF16),
            pltpu.VMEM((pairs, 2 * ny, nz), BF16),
            pltpu.VMEM((pairs, ny, nz), F32),
            pltpu.VMEM((4, ny, nz), F32),
            pltpu.VMEM((2, ny, nz), F32),
            pltpu.VMEM((4, ny, nz), F32),
            pltpu.VMEM((8, 128), F32),
            pltpu.VMEM((spaces, 8, 128), F32),
            pltpu.VMEM((8, 128), F32),
            pltpu.VMEM((samples, 8, 128), F32),
            dma((2, pairs, 2)), dma((2, pairs, 2)), dma, dma, dma,
            dma, dma((2, levels)), dma, dma((spaces // 2,)), dma,
            dma((spaces,)), dma((spaces,)), dma((spaces,)), dma((spaces,)),
            dma((samples,)), dma((samples,)),
        ],
        compiler_params=pltpu.CompilerParams(
            collective_id=0, has_side_effects=True, vmem_limit_bytes=60 * 1024 * 1024
        ),
    )(
        fine_state.astype(F32).reshape(pairs, slab, ny, nz),
        spectra, plane_assign, pack(partner_state), pack(coarse_state),
        jnp.stack([turbine_x, turbine_y, turbine_z]), thrust[None],
        jnp.asarray(zt), jnp.asarray(yt), jnp.asarray(zs), jnp.asarray(ys), jnp.asarray(rep),
    )
    return field.reshape(pairs, slab, ny * nz), unpack(partner), unpack(alone), est[0, :2]


def solution(mesh):
    return jax.shard_map(
        functools.partial(shards, mesh.shape["space"], mesh.shape["sample"]),
        mesh=mesh,
        in_specs=(
            P("sample", None, "space", None),
            P("sample", None),
            P("sample", "space", None),
            P("sample", None, None),
            P(("space", "sample"), None, None),
            P(),
            P(),
            P(),
            P(),
        ),
        out_specs=(
            P("sample", "space", None),
            P("sample", None, None),
            P(("space", "sample"), None, None),
            P(),
        ),
        check_vma=False,
    )
```

time: 248 us -> 106 us (0.43)
  Pallas kernels: 0 us -> 91.3 us
  waiting for transfers between devices: 61 us -> 0 us
  other arithmetic: 43.8 us -> 1.37 us
  blocking collectives: 39.4 us -> 0 us
  local copies, waits for them, and re-layouts: 48.3 us -> 11.8 us
  matrix products: 19.8 us -> 0 us
  starting transfers between devices: 18.3 us -> 0 us
  between operations: 16.6 us -> 0.71 us
    pallas_call x0 -> x1, Pallas kernels: none -> 91.3 us  [shards(): pl.pallas_call(functools.partial(kernel, spaces, samples, planes), out_sh...]
    psum x1 -> x0, waiting for transfers between devices: 61 us -> none  [shards(): fine_noise = lax.psum(partial_noise, 'space') * norm_scale]
    psum x1 -> x0, blocking collectives: 39.4 us -> none  [shards(): totals = lax.psum(partials, ('space', 'sample'))]
    dot_general x6 -> x0, matrix products: 19.8 us -> none  [the longest x2 8.14 us: drag_field(): jnp.dot(along_x.T, cross_mask, precision=HIGHEST)]
    reduce_sum x7 -> x0, other arithmetic: 16.8 us -> none  [the longest x2 11.1 us: restrict(): values.reshape(leading + (y_count // 8, 8, z_count // 8, 8))]
    reshape x10 -> x8, local copies, waits for them, and re-layouts: 25.8 us -> 10 us  [the longest x1 3.65 us: shards(): field.reshape(pairs, slab, ny * nz)]
    slice x32 -> x0, local copies, waits for them, and re-layouts: 11.3 us -> none  [the longest x6 4.29 us: advance(): jnp.roll(centre, -1, -1)]
    ppermute x4 -> x0, starting transfers between devices: 9.92 us -> none  [the longest x2 7.36 us: with_halo(): lax.ppermute(tail, axis, [(i, (i + 1) % count) for i in range(ends)])]
  transfers between devices with their start and end apart: 6 -> 0, of which waited for: 1 -> 0; matrix products, arithmetic and copies ran while one was open for 36% -> 0% of each run, Pallas kernels for 0% -> 0%
where the time goes in v1:
time: 106 us; the launch traced here: 105 us
  Pallas kernels  91.3 us (86%)
  local copies, waits for them, and re-layouts  11.8 us (11%)
  other arithmetic  1.37 us (1%)
    pallas_call x1, Pallas kernels, shards(): pl.pallas_call(functools.partial(kernel, spaces, samples, planes), out_sh...  91.3 us
    reshape x1, local copies, waits for them, and re-layouts, shards(): field.reshape(pairs, slab, ny * nz)  3.65 us
    reshape x4, local copies, waits for them, and re-layouts, pack(): state.reshape(-1, planes, yc, zc).transpose(0, 2, 1, 3)  3.25 us

profile of v1, /device:TPU:0, one launch (start us, length us, event | category | flops | bytes accessed | tf_op | source)
XLA Modules:
  0.0 105.2 jit_solution(9143059013058537454)
XLA Ops:
  0.6 0.0 copy-start
  0.6 1.4 %pad_add_fusion.turbines = s32[3,16]{1,0:T(4,128)} fusion(s32[1,16]{1,0:T(1,128)} %bitcast.29, s32[1,16]{1,0:T(1,128)} %bitcast.30, s32[1,16]{1,0:T(1,128)} %bitcast.31), kind=kLoop, calls=%fused_computation | loop fusion | flops 96 | bytes 384 | tf_op jit(solution)/shard_map/stack | solution.py:429
  2.0 0.9 reshape.44
  2.9 0.1 copy.23
  3.0 0.7 copy.25.coarse
  3.7 1.0 reshape.42
  4.6 0.1 copy.22
  4.8 0.7 copy.24.partner
  5.5 0.0 copy-done
  5.5 1.6 %reshape.52.fine_hbm = f32[2,2,512,256]{3,2,1,0:T(8,128)} reshape(bf16[2,2,131072]{2,1,0:T(2,128)(2,1)S(1)} %copy-done) | data formatting | bytes 3145728 | tf_op jit(solution)/shard_map/reshape | solution.py:427
  7.1 91.3 %shard_map.165 = (f32[2,2,512,256]{3,2,1,0:T(8,128)}, f32[2,64,128]{2,1,0:T(8,128)}, f32[1,64,128]{2,1,0:T(8,128)}, f32[8,128]{1,0:T(8,128)}) custom-call(f32[2,2,512,256]{3,2,1,0:T(8,128)} %reshape.52.fine_hbm, f32[18,2,32,256]{3,2,1,0:T(8,128)} %spec.1, s32[1,18]{1,0:T(1,128)} %assign.1, f32[2,64,128]{2,1,0:T(8,128)} %copy.24.partner, ...), custom_call_target="tpu_custom_call" | custom-call | tf_op jit(solution)/shard_map/pallas_call | solution.py:387
  98.4 0.0 copy-start.2
  98.4 0.0 copy-start.1
  98.4 3.7 %reshape.46 = f32[2,2,131072]{2,1,0:T(2,128)} reshape(f32[2,2,512,256]{3,2,1,0:T(8,128)} %get-tuple-element.8) | data formatting | bytes 4194304 | tf_op jit(solution)/shard_map/reshape | solution.py:432
  102.1 1.2 %slice_bitcast_fusion = f32[2]{0:T(128)} fusion(f32[8,128]{1,0:T(8,128)} %get-tuple-element.11), kind=kLoop, calls=%fused_computation.1 | loop fusion | bytes 16 | tf_op jit(solution)/shard_map/squeeze | solution.py:432
  103.2 0.0 copy-done.2
  103.3 0.1 copy.28
  103.3 0.1 copy.29
  103.5 0.7 reshape.50
  104.2 0.0 copy-done.1
  104.2 0.1 copy.26
  104.3 0.1 copy.27
  104.4 0.8 reshape.48
Async XLA Ops:
  0.6 4.8 %copy-start = (bf16[2,2,131072]{2,1,0:T(2,128)(2,1)S(1)}, bf16[2,2,131072]{2,1,0:T(2,128)(2,1)}, u32[]{:S(2)}) copy-start(bf16[2,2,131072]{2,1,0:T(2,128)(2,1)} %param.16) | copy-start | bytes 3145732
  98.4 4.9 %copy-start.2 = (f32[1,64,128]{2,1,0:T(8,128)S(1)}, f32[1,64,128]{2,1,0:T(8,128)}, u32[]{:S(2)}) copy-start(f32[1,64,128]{2,1,0:T(8,128)} %get-tuple-element.10) | copy-start | bytes 98308
  98.4 5.8 %copy-start.1 = (f32[2,64,128]{2,1,0:T(8,128)S(1)}, f32[2,64,128]{2,1,0:T(8,128)}, u32[]{:S(2)}) copy-start(f32[2,64,128]{2,1,0:T(8,128)} %get-tuple-element.9) | copy-start | bytes 196612

commit v2 on v1

--- a/solution.py
+++ b/solution.py
@@ -62,8 +62,8 @@
 
 
 def kernel(
-    spaces, samples, coarse_planes,
-    fine_hbm, spec, assign, partner, coarse, turbines, thrust, zt_hbm, yt_hbm, z_small, y_small,
+    spaces, samples,
+    fine_hbm, spec, assign, partner, coarse, tx_ref, ty_ref, tz_ref, thrust, zt_hbm, yt_hbm, z_small, y_small,
     rep, fine_out, partner_out, coarse_out, est_out,
     own, halo, block, gath, al_in, al_out, al_recv, zt, yt, pq_hi, pq_lo, g_ref, rk, kd, u1, part,
     parts, group, groups,
@@ -75,8 +75,9 @@
     last = spaces - 1
     pairs, _, ny, nz = fine_hbm.shape
     ky = spec.shape[2]
-    yc, width = coarse.shape[1], coarse.shape[2]
-    zc = width // coarse_planes
+    yc, zc = ny // 8, nz // 8
+    coarse_planes, cells = coarse.shape[1:]
+    width = 128
     core = lax.rem(me, 2)
     chip = me // 2
     across = lax.rem(chip, 2)
@@ -117,15 +118,14 @@
         return remote(fine_hbm.at[n, p], halo.at[1, n, p], halo_s.at[1, n, p], halo_r.at[1, n, p],
                       space=jnp.maximum(me - 1, 0))
 
-    @pl.when(me < last)
-    def _():
-        for n in range(pairs):
+    def start_halo(n):
+        @pl.when(me < last)
+        def _():
             for p in (1, 0):
                 to_right(n, p).start()
 
-    @pl.when(me > 0)
-    def _():
-        for n in range(pairs):
+        @pl.when(me > 0)
+        def _():
             for p in (0, 1):
                 to_left(n, p).start()
 
@@ -158,12 +158,26 @@
                       space=(k * 2 + across) * 2 + core)
 
     others(levels, level, lambda k: along(k, 0, block, chip).start())
+    for n in range(pairs - 1):
+        start_halo(n)
 
     z_out = dot_right(al_in[...], z_small[0], z_small[1])
     al_out[...] = z_out.reshape(spaces, ky, 2 * zc)
     al_recv[me] = al_out[me]
 
-    tx, ty, tz = turbines[0:1], turbines[1:2], turbines[2:3]
+    def got(c):
+        remote(block, gath.at[core, c], gx_s, g_r.at[c], space=dev_x).wait_recv()
+
+    got(chip_x)
+    others(levels, level, lambda k: along(k, 1, gath.at[core, chip_x], chip_x).start())
+
+    def send_alone(p):
+        return remote(al_out.at[p], al_recv.at[me], al_s.at[p], al_r.at[me], space=p)
+
+    others(spaces, me, lambda p: send_alone(p).start())
+    start_halo(pairs - 1)
+
+    tx, ty, tz = tx_ref[...], ty_ref[...], tz_ref[...]
     count = tx.shape[1]
 
     def cover(index, low, size):
@@ -180,24 +194,13 @@
             kd[j - 1] = drag
         rk[j] = 1.0 / (1.0 + drag)
 
-    def send_alone(p):
-        return remote(al_out.at[p], al_recv.at[me], al_s.at[p], al_r.at[me], space=p)
-
-    others(spaces, me, lambda p: send_alone(p).start())
-
-    cell = lax.broadcasted_iota(jnp.int32, (width, count), 0)
-    weight_c = jnp.where(tx // 8 == cell // zc, thrust[...], 0.0)
-    cover_zc = cover(cell % zc, tz, 1)
-    cover_yc = cover(lax.broadcasted_iota(jnp.int32, (yc, count), 0), ty, 1)
-    kc = lax.dot_general(cover_yc, cover_zc * weight_c, NT, precision=HIGHEST,
-                         preferred_element_type=F32)
+    cell = lax.broadcasted_iota(jnp.int32, (cells, count), 0)
+    at_x = lax.broadcasted_iota(jnp.int32, (coarse_planes, count), 0)
+    weight_c = jnp.where(tx // 8 == at_x, thrust[...], 0.0)
+    cover_c = cover(cell // zc, ty, 1) * cover(cell % zc, tz, 1)
+    kc = lax.dot_general(weight_c, cover_c, NT, precision=HIGHEST, preferred_element_type=F32)
     rkc = 1.0 / (1.0 + kc)
 
-    def got(c):
-        remote(block, gath.at[core, c], gx_s, g_r.at[c], space=dev_x).wait_recv()
-
-    got(chip_x)
-    others(levels, level, lambda k: along(k, 1, gath.at[core, chip_x], chip_x).start())
     others(levels, level, lambda k: got(k * 2 + across))
     others(levels, level, lambda k: got(k * 2 + 1 - across))
     send_c = remote(gath.at[core], gath.at[core], gc_s, gc_r, space=dev_c)
@@ -209,18 +212,28 @@
     folded = dot_left(y_small[0], y_small[1], al_recv[...].reshape(spaces * ky, 2 * zc))
     alone = jnp.dot(folded[0:yc], rep[0], precision=HIGHEST, preferred_element_type=F32) + jnp.dot(
         folded[yc : 2 * yc], rep[1], precision=HIGHEST, preferred_element_type=F32)
-    alone_g = 1.0 + (AMPLITUDE * norm) * alone
-
     lane = lax.broadcasted_iota(jnp.int32, (yc, width), 1)
-    z_at = lane % zc
+    row = lax.broadcasted_iota(jnp.int32, (yc, width), 0)
+    repeats = width // zc
+    fold = jnp.where(
+        lax.broadcasted_iota(jnp.int32, (yc // repeats, yc), 1) // repeats
+        == lax.broadcasted_iota(jnp.int32, (yc // repeats, yc), 0), 1.0, 0.0)
+
+    def flat(full):
+        kept = jnp.where(lane // zc == row % repeats, full, 0.0)
+        tiles = jnp.dot(fold, kept, precision=HIGHEST, preferred_element_type=F32)
+        return jnp.concatenate([tiles[j : j + 1] for j in range(yc // repeats)], axis=1)
+
+    alone_g = 1.0 + (AMPLITUDE * norm) * flat(alone)
+    z_at = lax.broadcasted_iota(jnp.int32, (coarse_planes, cells), 1) % zc
 
     def coarse_run(u, g):
         for _ in range(2):
-            west = jnp.where(z_at == 0, pltpu.roll(u, width - zc + 1, 1), pltpu.roll(u, 1, 1))
-            east = jnp.where(z_at == zc - 1, pltpu.roll(u, zc - 1, 1), pltpu.roll(u, width - 1, 1))
-            up = jnp.where(lane < zc, g, pltpu.roll(u, zc, 1))
-            down = jnp.where(lane >= width - zc, u, pltpu.roll(u, width - zc, 1))
-            side = west + east + pltpu.roll(u, 1, 0) + pltpu.roll(u, yc - 1, 0)
+            west = jnp.where(z_at == 0, pltpu.roll(u, cells - zc + 1, 1), pltpu.roll(u, 1, 1))
+            east = jnp.where(z_at == zc - 1, pltpu.roll(u, zc - 1, 1), pltpu.roll(u, cells - 1, 1))
+            up = jnp.concatenate([g, u[:-1]], axis=0)
+            down = jnp.concatenate([u[1:], u[-1:]], axis=0)
+            side = west + east + pltpu.roll(u, zc, 1) + pltpu.roll(u, cells - zc, 1)
             u = (0.05 * (u + g) + 0.4 * up + 0.1 * (down + side)) * rkc
         return u
 
@@ -264,7 +277,7 @@
     for n in range(pairs):
         gh, gl = split(g_ref[n] - 1.0)
         th, tl = split(dot(gh, mean_z) + dot(gl, mean_z))
-        partner_g = 1.0 + dot(mean_y, th) + dot(mean_y, tl)
+        partner_g = 1.0 + flat(dot(mean_y, th) + dot(mean_y, tl))
         run = coarse_run(partner[n], partner_g)
         partner_out[n] = run
         partner_power += jnp.sum(kc * run * run * run) * 0.25
@@ -333,8 +346,8 @@
     others(samples, sample, lambda p: remote(
         group, groups.at[p], q_s.at[p], q_r.at[p], sample=p).wait_recv())
     total = jnp.sum(groups[...], axis=0)
-    est_out[...] = jnp.where(lane8 == 0, total * (1.0 / (pairs * samples)),
-                             total * (1.0 / (spaces * samples)))
+    est_out[0] = jnp.sum(jnp.where(lane8 == 0, total, 0.0)) * (0.125 / (pairs * samples))
+    est_out[1] = jnp.sum(jnp.where(lane8 == 1, total, 0.0)) * (0.125 / (spaces * samples))
 
     @pl.when(me < last)
     def _():
@@ -367,34 +380,28 @@
     pairs, slab = fine_state.shape[:2]
     planes = partner_state.shape[1]
     yc, zc = ny // 8, nz // 8
-    width = planes * zc
+    cells = yc * zc
     levels = spaces // 4
     zt, yt, zs, ys = tables(spaces, ky, nz)
-    rep = np.zeros((2, 2 * zc, width), np.float32)
+    rep = np.zeros((2, 2 * zc, 128), np.float32)
     for c in range(2):
-        for x in range(planes):
-            rep[c, c * zc + np.arange(zc), x * zc + np.arange(zc)] = 1.0
-
-    def pack(state):
-        return state.reshape(-1, planes, yc, zc).transpose(0, 2, 1, 3).reshape(-1, yc, width)
-
-    def unpack(state):
-        return state.reshape(-1, yc, planes, zc).transpose(0, 2, 1, 3).reshape(-1, planes, yc * zc)
+        for at in range(128):
+            rep[c, c * zc + at % zc, at] = 1.0
 
     vmem = pl.BlockSpec(memory_space=pltpu.VMEM)
     anywhere = pl.BlockSpec(memory_space=pl.ANY)
     dma = pltpu.SemaphoreType.DMA
     field, partner, alone, est = pl.pallas_call(
-        functools.partial(kernel, spaces, samples, planes),
+        functools.partial(kernel, spaces, samples),
         out_shape=(
             jax.ShapeDtypeStruct((pairs, slab, ny, nz), F32),
-            jax.ShapeDtypeStruct((pairs, yc, width), F32),
-            jax.ShapeDtypeStruct((1, yc, width), F32),
-            jax.ShapeDtypeStruct((8, 128), F32),
+            jax.ShapeDtypeStruct((pairs, planes, cells), F32),
+            jax.ShapeDtypeStruct((1, planes, cells), F32),
+            jax.ShapeDtypeStruct((2,), F32),
         ),
-        in_specs=[anywhere, vmem, pl.BlockSpec(memory_space=pltpu.SMEM), vmem, vmem, vmem, vmem,
+        in_specs=[anywhere, vmem, pl.BlockSpec(memory_space=pltpu.SMEM)] + [vmem] * 6 + [
                   anywhere, anywhere, vmem, vmem, vmem],
-        out_specs=(vmem,) * 4,
+        out_specs=(vmem, vmem, vmem, pl.BlockSpec(memory_space=pltpu.SMEM)),
         scratch_shapes=[
             pltpu.VMEM((pairs, 2, ny, nz), F32),
             pltpu.VMEM((2, pairs, 2, ny, nz), F32),
@@ -425,11 +432,11 @@
         ),
     )(
         fine_state.astype(F32).reshape(pairs, slab, ny, nz),
-        spectra, plane_assign, pack(partner_state), pack(coarse_state),
-        jnp.stack([turbine_x, turbine_y, turbine_z]), thrust[None],
+        spectra, plane_assign, partner_state, coarse_state,
+        turbine_x[None], turbine_y[None], turbine_z[None], thrust[None],
         jnp.asarray(zt), jnp.asarray(yt), jnp.asarray(zs), jnp.asarray(ys), jnp.asarray(rep),
     )
-    return field.reshape(pairs, slab, ny * nz), unpack(partner), unpack(alone), est[0, :2]
+    return field.reshape(pairs, slab, ny * nz), partner, alone, est
 
 
 def solution(mesh):

time: 106 us -> 81.2 us (0.77)
  Pallas kernels: 91.3 us -> 72.3 us
  local copies, waits for them, and re-layouts: 11.8 us -> 8.05 us
  other arithmetic: 1.37 us -> 0 us
    pallas_call x1, Pallas kernels: 91.3 us -> 72.3 us  [shards(): pl.pallas_call(functools.partial(kernel, spaces, samples), out_shape=(jax...]
    reshape x7 -> x1, local copies, waits for them, and re-layouts: 8.42 us -> 3.64 us  [shards(): return (field.reshape(pairs, slab, ny * nz), partner, alone, est)]
    unnamed x6 -> x9, local copies, waits for them, and re-layouts: 0.01 us -> 1.77 us
    another operation x1 -> x0, other arithmetic: 1.37 us -> none  [shards(): jnp.stack([turbine_x, turbine_y, turbine_z])]
    squeeze x1 -> x0, local copies, waits for them, and re-layouts: 1.19 us -> none  [shards(): est[0, :2]]
where the time goes in v2:
time: 81.2 us; the launch traced here: 81 us
  Pallas kernels  72.3 us (89%)
  local copies, waits for them, and re-layouts  8.05 us (10%)
    pallas_call x1, Pallas kernels, shards(): pl.pallas_call(functools.partial(kernel, spaces, samples), out_shape=(jax...  72.3 us
    reshape x1, local copies, waits for them, and re-layouts, shards(): return (field.reshape(pairs, slab, ny * nz), partner, alone, est)  3.64 us
    reshape x1, local copies, waits for them, and re-layouts, shards(): fine_state.astype(F32).reshape(pairs, slab, ny, nz)  2.64 us
    unnamed x9, local copies, waits for them, and re-layouts  1.77 us

profile of v2, /device:TPU:0, one launch (start us, length us, event | category | flops | bytes accessed | tf_op | source)
XLA Modules:
  0.0 81.0 jit_solution(17037518284308867540)
XLA Ops:
  0.6 2.6 %reshape.20.fine_hbm = f32[2,2,512,256]{3,2,1,0:T(8,128)} reshape(bf16[2,2,131072]{2,1,0:T(2,128)(2,1)} %param.16) | data formatting | bytes 3145728 | tf_op jit(solution)/shard_map/reshape | solution.py:434
  3.3 72.3 %shard_map.165 = (f32[2,2,512,256]{3,2,1,0:T(8,128)}, f32[2,4,2048]{2,1,0:T(4,128)}, f32[1,4,2048]{2,1,0:T(4,128)}, f32[2]{0:T(128)}) custom-call(f32[2,2,512,256]{3,2,1,0:T(8,128)} %reshape.20.fine_hbm, f32[18,2,32,256]{3,2,1,0:T(8,128)} %spec.1, s32[1,18]{1,0:T(1,128)} %assign.1, f32[2,4,2048]{2,1,0:T(4,128)} %partner.1, f32[1,4,2048]{2,1,0:T(4,128)} %coarse.1, ...), custom_call_target="tpu_custom_call" | custom-call | tf_op jit(solution)/shard_map/pallas_call | solution.py:394
  75.6 0.0 copy-start
  75.6 0.0 copy-start.1
  75.6 0.0 copy-start.2
  75.6 3.6 %reshape.18 = f32[2,2,131072]{2,1,0:T(2,128)} reshape(f32[2,2,512,256]{3,2,1,0:T(8,128)} %get-tuple-element.8) | data formatting | bytes 4194304 | tf_op jit(solution)/shard_map/reshape | solution.py:439
  79.3 0.0 copy-done
  79.3 0.6 copy.21
  79.9 0.0 copy-done.1
  79.9 0.6 copy.22
  80.5 0.0 copy-done.2
  80.5 0.5 copy.23
Async XLA Ops:
  75.6 3.7 %copy-start = (f32[2,4,2048]{2,1,0:T(4,128)S(1)}, f32[2,4,2048]{2,1,0:T(4,128)}, u32[]{:S(2)}) copy-start(f32[2,4,2048]{2,1,0:T(4,128)} %get-tuple-element.17) | copy-start | bytes 196612
  75.6 4.3 %copy-start.1 = (f32[1,4,2048]{2,1,0:T(4,128)S(1)}, f32[1,4,2048]{2,1,0:T(4,128)}, u32[]{:S(2)}) copy-start(f32[1,4,2048]{2,1,0:T(4,128)} %get-tuple-element.18) | copy-start | bytes 98308
  75.6 4.9 %copy-start.2 = (f32[2]{0:T(128)S(1)}, f32[2]{0:T(128)}, u32[]{:S(2)}) copy-start(f32[2]{0:T(128)} %get-tuple-element.19) | copy-start | bytes 28

commit v3 on v2

--- a/solution.py
+++ b/solution.py
@@ -59,6 +59,14 @@
 def dot_left(high, low, x):
     xh, xl = split(x)
     return dot(high, xh) + dot(high, xl) + dot(low, xh)
+
+
+def over(x, size):
+    return lax.shift_right_logical(x, jnp.full_like(x, size.bit_length() - 1))
+
+
+def within(x, size):
+    return x & (size - 1)
 
 
 def kernel(
@@ -196,8 +204,8 @@
 
     cell = lax.broadcasted_iota(jnp.int32, (cells, count), 0)
     at_x = lax.broadcasted_iota(jnp.int32, (coarse_planes, count), 0)
-    weight_c = jnp.where(tx // 8 == at_x, thrust[...], 0.0)
-    cover_c = cover(cell // zc, ty, 1) * cover(cell % zc, tz, 1)
+    weight_c = jnp.where(over(tx, 8) == at_x, thrust[...], 0.0)
+    cover_c = cover(over(cell, zc), ty, 1) * cover(within(cell, zc), tz, 1)
     kc = lax.dot_general(weight_c, cover_c, NT, precision=HIGHEST, preferred_element_type=F32)
     rkc = 1.0 / (1.0 + kc)
 
@@ -216,16 +224,16 @@
     row = lax.broadcasted_iota(jnp.int32, (yc, width), 0)
     repeats = width // zc
     fold = jnp.where(
-        lax.broadcasted_iota(jnp.int32, (yc // repeats, yc), 1) // repeats
+        over(lax.broadcasted_iota(jnp.int32, (yc // repeats, yc), 1), repeats)
         == lax.broadcasted_iota(jnp.int32, (yc // repeats, yc), 0), 1.0, 0.0)
 
     def flat(full):
-        kept = jnp.where(lane // zc == row % repeats, full, 0.0)
+        kept = jnp.where(over(lane, zc) == within(row, repeats), full, 0.0)
         tiles = jnp.dot(fold, kept, precision=HIGHEST, preferred_element_type=F32)
         return jnp.concatenate([tiles[j : j + 1] for j in range(yc // repeats)], axis=1)
 
     alone_g = 1.0 + (AMPLITUDE * norm) * flat(alone)
-    z_at = lax.broadcasted_iota(jnp.int32, (coarse_planes, cells), 1) % zc
+    z_at = within(lax.broadcasted_iota(jnp.int32, (coarse_planes, cells), 1), zc)
 
     def coarse_run(u, g):
         for _ in range(2):
@@ -268,10 +276,10 @@
     lax.fori_loop(0, pairs * (ny // rows), y_stage, 0)
 
     mean_z = jnp.where(
-        lax.broadcasted_iota(jnp.int32, (nz, width), 0) // 8
-        == lax.broadcasted_iota(jnp.int32, (nz, width), 1) % zc, 0.125, 0.0).astype(BF16)
+        over(lax.broadcasted_iota(jnp.int32, (nz, width), 0), 8)
+        == within(lax.broadcasted_iota(jnp.int32, (nz, width), 1), zc), 0.125, 0.0).astype(BF16)
     mean_y = jnp.where(
-        lax.broadcasted_iota(jnp.int32, (yc, ny), 1) // 8
+        over(lax.broadcasted_iota(jnp.int32, (yc, ny), 1), 8)
         == lax.broadcasted_iota(jnp.int32, (yc, ny), 0), 0.125, 0.0).astype(BF16)
     partner_power = 0.0
     for n in range(pairs):
@@ -322,7 +330,8 @@
 
         for p in range(2):
             u = advance(u1[1 + p], u1[p], u1[2 + p], g, rk[1 + p])
-            fine_out[n, p] = u
+            for h in range(nz // 128):
+                fine_out[n, pl.ds(h * 2 + p, ny, stride=nz // 64), :] = u[:, h * 128 : h * 128 + 128]
             power += jnp.sum(kd[p] * u * u * u)
         return power
 
@@ -394,7 +403,7 @@
     field, partner, alone, est = pl.pallas_call(
         functools.partial(kernel, spaces, samples),
         out_shape=(
-            jax.ShapeDtypeStruct((pairs, slab, ny, nz), F32),
+            jax.ShapeDtypeStruct((pairs, slab * ny * nz // 128, 128), F32),
             jax.ShapeDtypeStruct((pairs, planes, cells), F32),
             jax.ShapeDtypeStruct((1, planes, cells), F32),
             jax.ShapeDtypeStruct((2,), F32),
@@ -436,6 +445,7 @@
         turbine_x[None], turbine_y[None], turbine_z[None], thrust[None],
         jnp.asarray(zt), jnp.asarray(yt), jnp.asarray(zs), jnp.asarray(ys), jnp.asarray(rep),
     )
+    field = field.reshape(pairs, ny * nz // 128, slab, 128).transpose(0, 2, 1, 3)
     return field.reshape(pairs, slab, ny * nz), partner, alone, est
 
 

time: 81.2 us -> 80.7 us (level)
    reshape x1 -> x0, local copies, waits for them, and re-layouts: 3.64 us -> none  [shards(): return (field.reshape(pairs, slab, ny * nz), partner, alone, est)]
    unnamed x9 -> x10, local copies, waits for them, and re-layouts: 1.77 us -> 4.83 us
where the time goes in v3:
time: 80.7 us; the launch traced here: 80.5 us
  Pallas kernels  72.3 us (90%)
  local copies, waits for them, and re-layouts  7.48 us (9%)
    pallas_call x1, Pallas kernels, shards(): pl.pallas_call(functools.partial(kernel, spaces, samples), out_shape=(jax...  72.3 us
    unnamed x10, local copies, waits for them, and re-layouts  4.83 us
    reshape x1, local copies, waits for them, and re-layouts, shards(): fine_state.astype(F32).reshape(pairs, slab, ny, nz)  2.64 us

profile of v3, /device:TPU:0, one launch (start us, length us, event | category | flops | bytes accessed | tf_op | source)
XLA Modules:
  0.0 80.5 jit_solution(9453863867585895247)
XLA Ops:
  0.6 2.6 %reshape.24.fine_hbm = f32[2,2,512,256]{3,2,1,0:T(8,128)} reshape(bf16[2,2,131072]{2,1,0:T(2,128)(2,1)} %param.16) | data formatting | bytes 3145728 | tf_op jit(solution)/shard_map/reshape | solution.py:443
  3.3 72.3 %shard_map.165 = (f32[2,2048,128]{2,1,0:T(8,128)}, f32[2,4,2048]{2,1,0:T(4,128)}, f32[1,4,2048]{2,1,0:T(4,128)}, f32[2]{0:T(128)}) custom-call(f32[2,2,512,256]{3,2,1,0:T(8,128)} %reshape.24.fine_hbm, f32[18,2,32,256]{3,2,1,0:T(8,128)} %spec.1, s32[1,18]{1,0:T(1,128)} %assign.1, f32[2,4,2048]{2,1,0:T(4,128)} %partner.1, f32[1,4,2048]{2,1,0:T(4,128)} %coarse.1, ...), custom_call_target="tpu_custom_call" | custom-call | tf_op jit(solution)/shard_map/pallas_call | solution.py:403
  75.6 0.0 copy-start
  75.6 0.0 copy-start.1
  75.6 0.0 copy-start.2
  75.6 3.1 %copy.23 = f32[2,2,131072]{2,1,0:T(2,128)} copy(f32[2,2,131072]{2,1,0:T(2,128)} %bitcast.9) | data formatting | bytes 4194304
  78.7 0.0 copy-done
  78.7 0.6 copy.24
  79.3 0.0 copy-done.1
  79.3 0.6 copy.25
  79.9 0.0 copy-done.2
  79.9 0.5 copy.26
Async XLA Ops:
  75.6 3.1 %copy-start = (f32[2,4,2048]{2,1,0:T(4,128)S(1)}, f32[2,4,2048]{2,1,0:T(4,128)}, u32[]{:S(2)}) copy-start(f32[2,4,2048]{2,1,0:T(4,128)} %get-tuple-element.17) | copy-start | bytes 196612
  75.6 3.7 %copy-start.1 = (f32[1,4,2048]{2,1,0:T(4,128)S(1)}, f32[1,4,2048]{2,1,0:T(4,128)}, u32[]{:S(2)}) copy-start(f32[1,4,2048]{2,1,0:T(4,128)} %get-tuple-element.18) | copy-start | bytes 98308
  75.6 4.3 %copy-start.2 = (f32[2]{0:T(128)S(1)}, f32[2]{0:T(128)}, u32[]{:S(2)}) copy-start(f32[2]{0:T(128)} %get-tuple-element.19) | copy-start | bytes 28

commit v4 on v3

--- a/solution.py
+++ b/solution.py
@@ -116,6 +116,10 @@
         barrier, inc=1, device_id={"space": i}, device_id_type=MESH))
     others(samples, sample, lambda i: pl.semaphore_signal(
         barrier, inc=1, device_id={"sample": i}, device_id_type=MESH))
+    for n in range(pairs):
+        planes = spec[assign[0, n]]
+        block[2 * n : 2 * n + 2] = planes
+        gath[core, chip, 2 * n : 2 * n + 2] = planes
     pl.semaphore_wait(barrier, spaces + samples - 2)
 
     def to_right(n, p):
@@ -136,6 +140,17 @@
         def _():
             for p in (0, 1):
                 to_left(n, p).start()
+
+    send_x = remote(block, gath.at[core, chip], gx_s, g_r.at[chip], space=dev_x)
+    send_x.start()
+
+    def along(k, which, src, chip_of):
+        return remote(src, gath.at[core, chip_of], gz_s.at[which, k], g_r.at[chip_of],
+                      space=(k * 2 + across) * 2 + core)
+
+    others(levels, level, lambda k: along(k, 0, block, chip).start())
+    for n in range(pairs - 1):
+        start_halo(n)
 
     zt_copy = pltpu.make_async_copy(zt_hbm, zt, zt_sem)
     yt_copy = pltpu.make_async_copy(yt_hbm, yt, yt_sem)
@@ -144,11 +159,6 @@
     yt_copy.start()
     own_copy.start()
 
-    for n in range(pairs):
-        planes = spec[assign[0, n]]
-        block[2 * n : 2 * n + 2] = planes
-        gath[core, chip, 2 * n : 2 * n + 2] = planes
-
     def stage(p, carry):
         planes = spec[assign[0, pairs + p]]
         rows = pl.ds(pl.multiple_of(p * ky, ky), ky)
@@ -158,19 +168,9 @@
 
     lax.fori_loop(0, spaces, stage, 0)
 
-    send_x = remote(block, gath.at[core, chip], gx_s, g_r.at[chip], space=dev_x)
-    send_x.start()
-
-    def along(k, which, src, chip_of):
-        return remote(src, gath.at[core, chip_of], gz_s.at[which, k], g_r.at[chip_of],
-                      space=(k * 2 + across) * 2 + core)
-
-    others(levels, level, lambda k: along(k, 0, block, chip).start())
-    for n in range(pairs - 1):
-        start_halo(n)
-
     z_out = dot_right(al_in[...], z_small[0], z_small[1])
-    al_out[...] = z_out.reshape(spaces, ky, 2 * zc)
+    z_out = z_out.reshape(spaces, ky, 2 * zc)
+    al_out[...] = jnp.concatenate([z_out[:, : ky // 2], z_out[:, ky // 2 :]], axis=2)
     al_recv[me] = al_out[me]
 
     def got(c):
@@ -217,7 +217,9 @@
     others(spaces, me, lambda p: remote(
         al_out.at[p], al_recv.at[p], al_s.at[p], al_r.at[p], space=p).wait_recv())
     norm = 1.0 / math.sqrt(ny * nz)
-    folded = dot_left(y_small[0], y_small[1], al_recv[...].reshape(spaces * ky, 2 * zc))
+    packed = al_recv[...]
+    packed = jnp.concatenate([packed[:, :, : 2 * zc], packed[:, :, 2 * zc :]], axis=1)
+    folded = dot_left(y_small[0], y_small[1], packed.reshape(spaces * ky, 2 * zc))
     alone = jnp.dot(folded[0:yc], rep[0], precision=HIGHEST, preferred_element_type=F32) + jnp.dot(
         folded[yc : 2 * yc], rep[1], precision=HIGHEST, preferred_element_type=F32)
     lane = lax.broadcasted_iota(jnp.int32, (yc, width), 1)
@@ -302,20 +304,15 @@
 
         @pl.when(me > 0)
         def _():
-            for p in (1, 0):
-                to_right(n, p).wait_recv()
-            u1[0] = advance(halo[0, n, 1], halo[0, n, 0], own[n, 0], g, rk[0])
+            to_right(n, 1).wait_recv()
 
         @pl.when(me == 0)
         def _():
             halo[0, n, 1] = g
-            u1[0] = g
 
         @pl.when(me < last)
         def _():
-            for p in (0, 1):
-                to_left(n, p).wait_recv()
-            u1[3] = advance(halo[1, n, 0], own[n, 1], halo[1, n, 1], g, rk[3])
+            to_left(n, 0).wait_recv()
 
         @pl.when(me == last)
         def _():
@@ -323,6 +320,20 @@
 
         u1[1] = advance(own[n, 0], halo[0, n, 1], own[n, 1], g, rk[1])
         u1[2] = advance(own[n, 1], own[n, 0], halo[1, n, 0], g, rk[2])
+
+        @pl.when(me > 0)
+        def _():
+            to_right(n, 0).wait_recv()
+            u1[0] = advance(halo[0, n, 1], halo[0, n, 0], own[n, 0], g, rk[0])
+
+        @pl.when(me == 0)
+        def _():
+            u1[0] = g
+
+        @pl.when(me < last)
+        def _():
+            to_left(n, 1).wait_recv()
+            u1[3] = advance(halo[1, n, 0], own[n, 1], halo[1, n, 1], g, rk[3])
 
         @pl.when(me == last)
         def _():
@@ -417,8 +428,8 @@
             pltpu.VMEM((2 * pairs, ky, nz), F32),
             pltpu.VMEM((2, spaces // 2, 2 * pairs, ky, nz), F32),
             pltpu.VMEM((spaces * ky, 2 * nz), F32),
-            pltpu.VMEM((spaces, ky, 2 * zc), F32),
-            pltpu.VMEM((spaces, ky, 2 * zc), F32),
+            pltpu.VMEM((spaces, ky // 2, 4 * zc), F32),
+            pltpu.VMEM((spaces, ky // 2, 4 * zc), F32),
             pltpu.VMEM(zt.shape, BF16),
             pltpu.VMEM(yt.shape, BF16),
             pltpu.VMEM((pairs, 2 * ny, nz), BF16),

time: 80.7 us -> 78 us (0.967)
  Pallas kernels: 72.3 us -> 69.7 us
    pallas_call x1, Pallas kernels: 72.3 us -> 69.7 us  [shards(): pl.pallas_call(functools.partial(kernel, spaces, samples), out_shape=(jax...]
where the time goes in v4:
time: 78 us; the launch traced here: 77.8 us
  Pallas kernels  69.7 us (89%)
  local copies, waits for them, and re-layouts  7.48 us (10%)
    pallas_call x1, Pallas kernels, shards(): pl.pallas_call(functools.partial(kernel, spaces, samples), out_shape=(jax...  69.7 us
    unnamed x10, local copies, waits for them, and re-layouts  4.83 us
    reshape x1, local copies, waits for them, and re-layouts, shards(): fine_state.astype(F32).reshape(pairs, slab, ny, nz)  2.64 us

profile of v4, /device:TPU:0, one launch (start us, length us, event | category | flops | bytes accessed | tf_op | source)
XLA Modules:
  0.0 77.8 jit_solution(7116179371197148021)
XLA Ops:
  0.6 2.6 %reshape.24.fine_hbm = f32[2,2,512,256]{3,2,1,0:T(8,128)} reshape(bf16[2,2,131072]{2,1,0:T(2,128)(2,1)} %param.16) | data formatting | bytes 3145728 | tf_op jit(solution)/shard_map/reshape | solution.py:454
  3.3 69.7 %shard_map.165 = (f32[2,2048,128]{2,1,0:T(8,128)}, f32[2,4,2048]{2,1,0:T(4,128)}, f32[1,4,2048]{2,1,0:T(4,128)}, f32[2]{0:T(128)}) custom-call(f32[2,2,512,256]{3,2,1,0:T(8,128)} %reshape.24.fine_hbm, f32[18,2,32,256]{3,2,1,0:T(8,128)} %spec.1, s32[1,18]{1,0:T(1,128)} %assign.1, f32[2,4,2048]{2,1,0:T(4,128)} %partner.1, f32[1,4,2048]{2,1,0:T(4,128)} %coarse.1, ...), custom_call_target="tpu_custom_call" | custom-call | tf_op jit(solution)/shard_map/pallas_call | solution.py:414
  73.0 0.0 copy-start
  73.0 0.0 copy-start.1
  73.0 0.0 copy-start.2
  73.0 3.1 %copy.23 = f32[2,2,131072]{2,1,0:T(2,128)} copy(f32[2,2,131072]{2,1,0:T(2,128)} %bitcast.9) | data formatting | bytes 4194304
  76.1 0.0 copy-done
  76.1 0.6 copy.24
  76.7 0.0 copy-done.1
  76.7 0.6 copy.25
  77.3 0.0 copy-done.2
  77.3 0.5 copy.26
Async XLA Ops:
  73.0 3.1 %copy-start = (f32[2,4,2048]{2,1,0:T(4,128)S(1)}, f32[2,4,2048]{2,1,0:T(4,128)}, u32[]{:S(2)}) copy-start(f32[2,4,2048]{2,1,0:T(4,128)} %get-tuple-element.17) | copy-start | bytes 196612
  73.0 3.7 %copy-start.1 = (f32[1,4,2048]{2,1,0:T(4,128)S(1)}, f32[1,4,2048]{2,1,0:T(4,128)}, u32[]{:S(2)}) copy-start(f32[1,4,2048]{2,1,0:T(4,128)} %get-tuple-element.18) | copy-start | bytes 98308
  73.0 4.3 %copy-start.2 = (f32[2]{0:T(128)S(1)}, f32[2]{0:T(128)}, u32[]{:S(2)}) copy-start(f32[2]{0:T(128)} %get-tuple-element.19) | copy-start | bytes 28
